TPU v7x, 32 devices: a whole 2x2x4 slice. The times are simulated.
32 devices in a mesh: seq: 8 (over z, y), head: 4 (over x, core).
Axes of the slice: x: 2, y: 2, z: 4, core: 2. Of those that a mesh axis runs over, the one named last changes fastest.
Arguments:
- tokens: bfloat16 [2048, 1024], P('seq'), may hold values from -6 to 6
- w_qkv: bfloat16 [1024, 3, 1024], P('seq', None, 'head'), may hold values from -0.1875 to 0.1875
- w_out: bfloat16 [1024, 1024], P('head', 'seq'), may hold values from -1 to 1
- ln1_gain: bfloat16 [1024], P('seq'), may hold values from 0.5 to 1.5
- ln1_bias: bfloat16 [1024], P('seq'), may hold values from -1.796875 to 1.796875
- ln2_gain: bfloat16 [1024], P('seq'), may hold values from 0.5 to 1.5
- ln2_bias: bfloat16 [1024], P('seq'), may hold values from -1.796875 to 1.796875
- w_up: bfloat16 [1024, 4096], P('seq', 'head'), may hold values from -0.1875 to 0.1875
- up_bias: bfloat16 [4096], P('head'), may hold values from -1.796875 to 1.796875
- w_down: bfloat16 [4096, 1024], P('head', 'seq'), may hold values from -0.09375 to 0.09375
- down_bias: bfloat16 [1024], P('seq'), may hold values from -1.796875 to 1.796875
- seq_units: int32 [4], replicated, may hold values from 1 to 4, 8 in all
- seq_pad: int32 [4], replicated, may hold values from 0 to 127
- rand_picks: int32 [32, 16, 3], P('seq', 'head'), may hold values from 0 to 65535
- cotangent: bfloat16 [2048, 1024], P('seq'), may hold values from -6 to 6
Outputs:
- output: bfloat16 [2048, 1024], P('seq')
- x_grad: float32 [2048, 1024], P('seq')
- w_qkv_grad: float32 [1024, 3, 1024], P('seq', None, 'head')
- w_out_grad: float32 [1024, 1024], P('head', 'seq')
- ln1_gain_grad: float32 [1024], P('seq')
- ln1_bias_grad: float32 [1024], P('seq')
- ln2_gain_grad: float32 [1024], P('seq')
- ln2_bias_grad: float32 [1024], P('seq')
- w_up_grad: float32 [1024, 4096], P('seq', 'head')
- up_bias_grad: float32 [4096], P('head')
- w_down_grad: float32 [4096, 1024], P('head', 'seq')
- down_bias_grad: float32 [1024], P('seq')
Inputs may be any that keep to these rules, and one draw needn't show every extreme that they name: `seq_units`: each sequence covers whole units; the values add up to the number of units in the stream, and some sequence covers 4 units.
All inputs are finite; a program needn't handle non-finite values.
Results may differ from a plain program's by a relative error of at most 0.012.
Values may be sent and summed in bfloat16 or wider, within the bound.
A program may use at most 128 MiB of HBM per device.

v0:
```python
import jax
import jax.numpy as jnp
from jax import lax
from jax.sharding import PartitionSpec as P

HEAD_DIM = 64
BLK = 64
SPAN = 4
BLK_DEV = 4
EPSILON = 1e-05
NEGATIVE = -1e30
F32 = jnp.float32
BF16 = jnp.bfloat16


def shifted(value, axis, steps):
    count = lax.axis_size(axis)
    first, last = (max(0, -steps), min(count, count - steps))
    return lax.ppermute(value, axis, [(i, i + steps) for i in range(first, last)])


def norm_parts(features):
    average = jnp.mean(features, axis=-1, keepdims=True)
    centred = features - average
    spread = jnp.mean(centred * centred, axis=-1, keepdims=True)
    inverse = lax.rsqrt(spread + EPSILON)
    return (centred * inverse, inverse)


def norm_backward(xhat, inverse, scaled):
    first = jnp.mean(scaled, axis=-1, keepdims=True)
    second = jnp.mean(scaled * xhat, axis=-1, keepdims=True)
    return inverse * (scaled - first - xhat * second)


def dot(a, b, dims):
    return lax.dot_general(a, b, (dims, ((), ())), preferred_element_type=F32)


def sequence_place(seq_units, seq_pad):
    device = lax.axis_index("seq")
    start, leader, span, pad = (0, 0, 0, 0)
    for k in range(seq_units.shape[0]):
        units = seq_units[k]
        inside = (device >= start) & (device < start + units)
        leader = jnp.where(inside, start, leader)
        span = jnp.where(inside, units, span)
        pad = jnp.where(inside, seq_pad[k], pad)
        start = start + units
    return (device - leader, span, pad)


def key_counts(position, span, picks):
    blocks = lax.broadcasted_iota(jnp.int32, (1, 1, SPAN * BLK_DEV), 2)
    query = position * BLK_DEV + lax.broadcasted_iota(jnp.int32, (BLK_DEV, 1, 1), 0)
    total = span * BLK_DEV
    count = jnp.zeros((BLK_DEV, picks.shape[1], SPAN * BLK_DEV), F32)
    for wanted in (query - 1, query, query + 1, 0, total - 1):
        count = count + (blocks == wanted).astype(F32)
    chosen = picks % total
    for r in range(picks.shape[2]):
        count = count + (blocks == chosen[:, :, r : r + 1]).astype(F32)
    return jnp.where((query == 0) | (query == total - 1), 1.0, count)


def local_general(
    tokens,
    w_qkv,
    w_out,
    ln1_gain,
    ln1_bias,
    ln2_gain,
    ln2_bias,
    w_up,
    up_bias,
    w_down,
    down_bias,
    seq_units,
    seq_pad,
    rand_picks,
    cotangent,
):
    tok, width = tokens.shape
    heads = w_qkv.shape[2] // HEAD_DIM
    rows = lambda v: lax.all_gather(v, "seq", axis=0, tiled=True)
    cols = lambda v: lax.all_gather(v, "seq", axis=1, tiled=True)
    vectors = jnp.stack([ln1_gain, ln1_bias, ln2_gain, ln2_bias, down_bias], axis=0)
    gain_one, shift_one, gain_two, shift_two, down_shift = [
        v[None].astype(F32) for v in cols(vectors)
    ]
    qkv = rows(w_qkv)
    out_w, up_w, down_w = (cols(w_out), rows(w_up), cols(w_down))
    position, span, pad = sequence_place(seq_units, seq_pad)
    root = SPAN - 1 - position
    inputs = tokens.astype(F32)
    xhat_one, inv_one = norm_parts(inputs)
    normed = (xhat_one * gain_one + shift_one).astype(BF16)
    triple = jnp.einsum("td,dcf->tcf", normed, qkv, preferred_element_type=F32).astype(BF16)
    own = jnp.stack([triple[:, 1], triple[:, 2]], axis=0)
    pieces = [own if o == 0 else shifted(own, "seq", -o) for o in range(1 - SPAN, SPAN)]
    nearby = jnp.stack(pieces, axis=0)
    window = lax.dynamic_slice_in_dim(nearby, root, SPAN, 0)
    split = lambda v: v.reshape(v.shape[0], heads, HEAD_DIM)
    keys = split(window[:, 0].reshape(SPAN * tok, -1))
    values = split(window[:, 1].reshape(SPAN * tok, -1))
    queries = split(triple[:, 0])
    scaling = HEAD_DIM ** (-0.5)
    live = jnp.arange(SPAN * tok, dtype=jnp.int32) < span * tok - pad
    count = jnp.repeat(key_counts(position, span, rand_picks), BLK, axis=2)
    count = jnp.where(live[None, None], count, 0.0)
    count = jnp.transpose(jnp.repeat(count, BLK, axis=0), (1, 0, 2))
    logits = jnp.einsum("qhd,khd->hqk", queries, keys, preferred_element_type=F32) * scaling
    logits = jnp.where(count > 0, logits, NEGATIVE)
    grown = jnp.exp(logits - jnp.max(logits, axis=-1, keepdims=True)) * count
    chances = grown / jnp.sum(grown, axis=-1, keepdims=True)
    chances_low = chances.astype(BF16)
    attended = jnp.einsum("hqk,khd->qhd", chances_low, values, preferred_element_type=F32)
    attended = attended.astype(BF16).reshape(tok, heads * HEAD_DIM)
    middle = inputs + lax.psum(dot(attended, out_w, ((1,), (0,))), "head")
    xhat_two, inv_two = norm_parts(middle)
    normed_two = (xhat_two * gain_two + shift_two).astype(BF16)
    pre_act = dot(normed_two, up_w, ((1,), (0,))) + up_bias.astype(F32)[None]
    hidden, pull = jax.vjp(lambda v: jax.nn.gelu(v, approximate=True), pre_act)
    hidden = hidden.astype(BF16)
    ffn = lax.psum(dot(hidden, down_w, ((1,), (0,))).astype(BF16), "head").astype(F32)
    output = (middle + ffn + down_shift).astype(BF16)
    grad_out = cotangent.astype(F32)
    grad_w_down = dot(hidden, cotangent, ((0,), (0,)))
    grad_pre = pull(dot(cotangent, down_w, ((1,), (1,))))[0].astype(BF16)
    grad_w_up = dot(normed_two, grad_pre, ((0,), (0,)))
    grad_up_bias = lax.psum(jnp.sum(grad_pre.astype(F32), axis=0), "seq")
    grad_two = lax.psum(dot(grad_pre, up_w, ((1,), (1,))), "head")
    grad_middle = grad_out + norm_backward(xhat_two, inv_two, grad_two * gain_two)
    grad_branch = grad_middle.astype(BF16)
    grad_w_out = dot(attended, grad_branch, ((0,), (0,)))
    grad_att = split(dot(grad_branch, out_w, ((1,), (1,))).astype(BF16))
    grad_prob = jnp.einsum("qhd,khd->hqk", grad_att, values, preferred_element_type=F32)
    inner = jnp.sum(chances * grad_prob, axis=-1, keepdims=True)
    grad_logit = (chances * (grad_prob - inner)).astype(BF16)
    dq = scaling * jnp.einsum("hqk,khd->qhd", grad_logit, keys, preferred_element_type=F32)
    dk = scaling * jnp.einsum("hqk,qhd->khd", grad_logit, queries, preferred_element_type=F32)
    dv = jnp.einsum("hqk,qhd->khd", chances_low, grad_att, preferred_element_type=F32)
    part = jnp.stack([dk.reshape(SPAN, tok, -1), dv.reshape(SPAN, tok, -1)], axis=1)
    near = jnp.zeros((2 * SPAN - 1,) + part.shape[1:], F32)
    near = lax.dynamic_update_slice_in_dim(near, part, root, 0)
    owned = near[SPAN - 1]
    for offset in range(1 - SPAN, SPAN):
        if offset:
            owned = owned + shifted(near[offset + SPAN - 1], "seq", offset)
    owned = owned.astype(BF16)
    grad_triple = jnp.stack([dq.reshape(tok, -1).astype(BF16), owned[0], owned[1]], axis=1)
    grad_w_qkv = jnp.einsum("td,tcf->dcf", normed, grad_triple, preferred_element_type=F32)
    grad_one = lax.psum(
        jnp.einsum("tcf,dcf->td", grad_triple, qkv, preferred_element_type=F32), "head"
    )
    x_grad = grad_middle + norm_backward(xhat_one, inv_one, grad_one * gain_one)
    sums = jnp.stack(
        [
            jnp.sum(grad_one * xhat_one, axis=0),
            jnp.sum(grad_one, axis=0),
            jnp.sum(grad_two * xhat_two, axis=0),
            jnp.sum(grad_two, axis=0),
            jnp.sum(grad_out, axis=0),
        ],
        axis=0,
    )
    scatter = lambda v, d: lax.psum_scatter(v, "seq", scatter_dimension=d, tiled=True)
    sums = scatter(sums, 1)
    return (
        output,
        x_grad,
        scatter(grad_w_qkv, 0),
        scatter(grad_w_out, 1),
        sums[0],
        sums[1],
        sums[2],
        sums[3],
        scatter(grad_w_up, 0),
        grad_up_bias,
        scatter(grad_w_down, 1),
        sums[4],
    )


IN_SPECS = (
    P("seq", None),
    P("seq", None, "head"),
    P("head", "seq"),
    P("seq"),
    P("seq"),
    P("seq"),
    P("seq"),
    P("seq", "head"),
    P("head"),
    P("head", "seq"),
    P("seq"),
    P(),
    P(),
    P("seq", "head", None),
    P("seq", None),
)
OUT_SPECS = (
    P("seq", None),
    P("seq", None),
    P("seq", None, "head"),
    P("head", "seq"),
    P("seq"),
    P("seq"),
    P("seq"),
    P("seq"),
    P("seq", "head"),
    P("head"),
    P("head", "seq"),
    P("seq"),
)


def solution(mesh):
    return jax.shard_map(
        local_general, mesh=mesh, in_specs=IN_SPECS, out_specs=OUT_SPECS, check_vma=False
    )
```

profile of v0, /device:TPU:0, one launch (start us, length us, event | category | flops | bytes accessed | tf_op | source)
XLA Modules:
  0.0 851.5 jit_solution(9352380124314227854)
XLA Ops:
  23.5 27.9 %all_gather.15 = bf16[5,1024]{1,0:T(8,128)(2,1)S(1)} all-gather(bf16[5,128]{1,0:T(8,128)(2,1)S(1)} %stack.75), channel_id=1, replica_groups=mesh['seq'=8,'head'=4] {'seq'}, dimensions={1}, use_global_device_ids=true | all-gather | bytes 11520 | tf_op jit(solution)/shard_map/all_gather | solution.py:86
  54.2 27.8 %all_gather.17 = bf16[256,1024]{1,0:T(8,128)(2,1)S(1)} all-gather(bf16[256,128]{1,0:T(8,128)(2,1)} %param.17), channel_id=1, replica_groups=mesh['seq'=8,'head'=4] {'seq'}, dimensions={1}, use_global_device_ids=true | all-gather | bytes 589824 | tf_op jit(solution)/shard_map/all_gather | solution.py:86
  86.1 5.1 collective-permute-start.1
  96.8 4.2 collective-permute-done.3
  101.0 6.9 collective-permute-done.4
  109.7 2.9 fusion.49
  113.3 3.2 convolution_convert_fusion.3
  119.3 38.9 %all-reduce.5.cloned.1.call-done = f32[256,1024]{1,0:T(8,128)} async-done(((f32[256,1024]{1,0:T(8,128)}), f32[256,1024]{1,0:T(8,128)}) %all-reduce.5.cloned.1.call-update) | async-done | bytes 1048592 | tf_op jit(solution)/shard_map/psum | solution.py:119
  159.9 52.1 %all-gather.8.cloned.1.call-done = bf16[1024,1024]{1,0:T(8,128)(2,1)} async-done(((bf16[1024,128]{1,0:T(8,128)(2,1)}), bf16[1024,1024]{1,0:T(8,128)(2,1)}) %all-gather.8.cloned.1.call-update) | async-done | bytes 2097168 | tf_op jit(solution)/shard_map/all_gather | solution.py:86
  211.9 3.3 fusion.51
  215.2 46.4 %all-gather.6.cloned.1.call-done = bf16[1024,1024]{1,0:T(8,128)(2,1)} async-done(((bf16[128,1024]{1,0:T(8,128)(2,1)}), bf16[1024,1024]{1,0:T(8,128)(2,1)}) %all-gather.6.cloned.1.call-update) | async-done | bytes 2097168 | tf_op jit(solution)/shard_map/all_gather | solution.py:85
  261.6 3.5 convert_reduce_fusion.2
  267.8 3.2 convolution_convert_fusion
  271.2 31.2 %all-reduce.9.cloned.1.call-done = f32[256,1024]{1,0:T(8,128)} async-done(((f32[256,1024]{1,0:T(8,128)}), f32[256,1024]{1,0:T(8,128)}) %all-reduce.9.cloned.1.call-update) | async-done | bytes 1048592 | tf_op jit(solution)/shard_map/psum | solution.py:132
  304.2 34.6 %all-reduce.7.cloned.1.call-done = bf16[256,1024]{1,0:T(8,128)(2,1)} async-done(((bf16[256,1024]{1,0:T(8,128)(2,1)}), bf16[256,1024]{1,0:T(8,128)(2,1)}) %all-reduce.7.cloned.1.call-update) | async-done | bytes 524304 | tf_op jit(solution)/shard_map/psum | solution.py:125
  338.8 2.9 convert_add_fusion.1
  363.6 4.2 collective-permute-start.10
  367.8 4.3 collective-permute-start.11
  375.9 3.4 collective-permute-done.10
  379.3 4.2 collective-permute-start.9
  384.4 11.5 %collective-permute-done.11 = f32[2,256,256]{2,1,0:T(8,128)} collective-permute-done((f32[2,256,256]{2,1,0:T(8,128)}, f32[2,256,256]{2,1,0:T(8,128)}, u32[]{:S(2)}, u32[]{:S(2)}) %collective-permute-start.11) | collective-permute-done | bytes 524320 | tf_op jit(solution)/shard_map/ppermute | solution.py:19
  395.9 5.4 collective-permute-done.7
  401.3 10.7 %collective-permute-done.9 = f32[2,256,256]{2,1,0:T(8,128)} collective-permute-done((f32[2,256,256]{2,1,0:T(8,128)}, f32[2,256,256]{2,1,0:T(8,128)}, u32[]{:S(2)}, u32[]{:S(2)}) %collective-permute-start.9) | collective-permute-done | bytes 524320 | tf_op jit(solution)/shard_map/ppermute | solution.py:19
  415.9 41.7 %all-reduce.11.cloned.1.call-done = f32[256,1024]{1,0:T(8,128)} async-done(((f32[256,1024]{1,0:T(8,128)}), f32[256,1024]{1,0:T(8,128)}) %all-reduce.11.cloned.1.call-update) | async-done | bytes 1048592 | tf_op jit(solution)/shard_map/psum | solution.py:153
  465.0 2.8 fusion.43
  469.2 2.9 fusion.42
  472.1 22.1 %psum.39 = f32[1024]{0:T(1024)} all-reduce(f32[1024]{0:T(1024)S(1)} %get-tuple-element.20), channel_id=1, replica_groups=mesh['seq'=8,'head'=4] {'seq'}, use_global_device_ids=true, to_apply=%region_25.26 | all-reduce | flops 1024 | bytes 8192 | tf_op jit(solution)/shard_map/psum | solution.py:131
  495.5 19.4 %reduce-scatter.10.cloned.1.call-done = f32[5,128]{1,0:T(8,128)} async-done(((f32[5,1024]{1,0:T(8,128)}), f32[5,128]{1,0:T(8,128)}) %reduce-scatter.10.cloned.1.call-update) | async-done | bytes 2576 | tf_op jit(solution)/shard_map/reduce_scatter | solution.py:167
  516.3 65.9 %reduce-scatter.8.cloned.1.call-done = f32[256,128]{1,0:T(8,128)} async-done(((f32[256,1024]{1,0:T(8,128)}), f32[256,128]{1,0:T(8,128)}) %reduce-scatter.8.cloned.1.call-update) | async-done | bytes 131088 | tf_op jit(solution)/shard_map/reduce_scatter | solution.py:167
  582.2 78.2 %reduce-scatter.6.cloned.1.call-done = f32[128,3,256]{2,0,1:T(8,128)} async-done(((f32[1024,3,256]{2,0,1:T(8,128)}), f32[128,3,256]{2,0,1:T(8,128)}) %reduce-scatter.6.cloned.1.call-update) | async-done | bytes 393232 | tf_op jit(solution)/shard_map/reduce_scatter | solution.py:167
  660.4 91.4 %reduce-scatter.12.cloned.1.call-done = f32[128,1024]{1,0:T(8,128)} async-done(((f32[1024,1024]{1,0:T(8,128)}), f32[128,1024]{1,0:T(8,128)}) %reduce-scatter.12.cloned.1.call-update) | async-done | bytes 524304 | tf_op jit(solution)/shard_map/reduce_scatter | solution.py:167
  751.8 92.8 %reduce-scatter.14.cloned.1.call-done = f32[1024,128]{1,0:T(8,128)} async-done(((f32[1024,1024]{1,0:T(8,128)}), f32[1024,128]{1,0:T(8,128)}) %reduce-scatter.14.cloned.1.call-update) | async-done | bytes 524304 | tf_op jit(solution)/shard_map/reduce_scatter | solution.py:167
  (156 shorter events, 71.9 us)
Async XLA Ops:
  7.2 74.8 %copy-start = (bf16[256,1024]{1,0:T(8,128)(2,1)S(1)}, bf16[256,1024]{1,0:T(8,128)(2,1)}, u32[]{:S(2)}) copy-start(bf16[256,1024]{1,0:T(8,128)(2,1)} %param.15) | copy-start | bytes 1572868
  7.2 74.8 %all-gather.4.cloned.1.call-start = ((), (), s32[]{:S(2)}) async-start(), calls=%async_computation.5 | async-start | bytes 1769472 | tf_op jit(solution)/shard_map/all_gather | solution.py:85
  9.0 149.2 %all-reduce.5.cloned.1.call-start = ((), (), s32[]{:S(2)}) async-start(), calls=%async_computation.6 | async-start | bytes 2097152 | tf_op jit(solution)/shard_map/psum | solution.py:119
  84.2 11.1 %collective-permute-start = (bf16[2,256,256]{1,2,0:T(8,128)(2,1)S(1)}, bf16[2,256,256]{1,2,0:T(8,128)(2,1)S(1)}, u32[]{:S(2)}, u32[]{:S(2)}) collective-permute-start(bf16[2,256,256]{1,2,0:T(8,128)(2,1)S(1)} %pad_maximum_fusion.1), channel_id=1, source_target_pairs={{0,12},{4,16},{8,20},{12,24},{16,28},{1,13},{5,17},{9,21},{13,25},... | collective-permute-start | bytes 786440 | tf_op jit(solution)/shard_map/ppermute | solution.py:19
  86.1 10.6 %collective-permute-start.1 = (bf16[2,256,256]{1,2,0:T(8,128)(2,1)S(1)}, bf16[2,256,256]{1,2,0:T(8,128)(2,1)S(1)}, u32[]{:S(2)}, u32[]{:S(2)}) collective-permute-start(bf16[2,256,256]{1,2,0:T(8,128)(2,1)S(1)} %pad_maximum_fusion.1), channel_id=1, source_target_pairs={{0,8},{4,12},{8,16},{12,20},{16,24},{20,28},{1,9},{5,13},{9,17},{1... | collective-permute-start | bytes 786440 | tf_op jit(solution)/shard_map/ppermute | solution.py:19
  91.3 5.4 collective-permute-start.2
  92.7 8.3 collective-permute-start.3
  94.0 13.9 %collective-permute-start.4 = (bf16[2,256,256]{1,2,0:T(8,128)(2,1)S(1)}, bf16[2,256,256]{1,2,0:T(8,128)(2,1)S(1)}, u32[]{:S(2)}, u32[]{:S(2)}) collective-permute-start(bf16[2,256,256]{1,2,0:T(8,128)(2,1)S(1)} %pad_maximum_fusion.1), channel_id=1, source_target_pairs={{8,0},{12,4},{16,8},{20,12},{24,16},{28,20},{9,1},{13,5},{17,9},{2... | collective-permute-start | bytes 786440 | tf_op jit(solution)/shard_map/ppermute | solution.py:19
  95.3 12.6 %collective-permute-start.5 = (bf16[2,256,256]{1,2,0:T(8,128)(2,1)S(1)}, bf16[2,256,256]{1,2,0:T(8,128)(2,1)S(1)}, u32[]{:S(2)}, u32[]{:S(2)}) collective-permute-start(bf16[2,256,256]{1,2,0:T(8,128)(2,1)S(1)} %pad_maximum_fusion.1), channel_id=1, source_target_pairs={{12,0},{16,4},{20,8},{24,12},{28,16},{13,1},{17,5},{21,9},{25,13},... | collective-permute-start | bytes 786440 | tf_op jit(solution)/shard_map/ppermute | solution.py:19
  117.9 94.0 %copy-start.7 = (bf16[256,1024]{1,0:T(8,128)(2,1)S(1)}, bf16[256,1024]{1,0:T(8,128)(2,1)}, u32[]{:S(2)}) copy-start(bf16[256,1024]{1,0:T(8,128)(2,1)} %param.29) | copy-start | bytes 1572868
  117.9 94.0 %all-gather.8.cloned.1.call-start = ((), (), s32[]{:S(2)}) async-start(), calls=%async_computation.8 | async-start | bytes 2359296 | tf_op jit(solution)/shard_map/all_gather | solution.py:86
  118.6 143.0 %all-gather.6.cloned.1.call-start = ((), (), s32[]{:S(2)}) async-start(), calls=%async_computation.7 | async-start | bytes 2359296 | tf_op jit(solution)/shard_map/all_gather | solution.py:85
  119.2 183.2 %all-reduce.9.cloned.1.call-start = ((), (), s32[]{:S(2)}) async-start(), calls=%async_computation.10 | async-start | bytes 2097152 | tf_op jit(solution)/shard_map/psum | solution.py:132
  261.6 4.3 copy-start.12
  267.7 71.1 %all-reduce.7.cloned.1.call-start = ((), (), s32[]{:S(2)}) async-start(), calls=%async_computation.9 | async-start | bytes 1048576 | tf_op jit(solution)/shard_map/psum | solution.py:125
  271.0 186.6 %all-reduce.11.cloned.1.call-start = ((), (), s32[]{:S(2)}) async-start(), calls=%async_computation.11 | async-start | bytes 2097152 | tf_op jit(solution)/shard_map/psum | solution.py:153
  338.8 3.3 copy-start.19
  360.6 22.9 %copy-start.2 = (bf16[4,256,1024]{2,1,0:T(8,128)(2,1)S(1)}, bf16[4,256,1024]{2,1,0:T(8,128)(2,1)}, u32[]{:S(2)}) copy-start(bf16[4,256,1024]{2,1,0:T(8,128)(2,1)} %copy-done.1) | copy-start | bytes 6291460
  360.6 22.9 %copy-start.6 = (bf16[1024,4,64]{0,2,1:T(8,128)(2,1)S(1)}, bf16[1024,4,64]{0,2,1:T(8,128)(2,1)}, u32[]{:S(2)}) copy-start(bf16[1024,4,64]{0,2,1:T(8,128)(2,1)} %copy-done.5) | copy-start | bytes 1572868
  363.6 15.7 %collective-permute-start.10 = (f32[2,256,256]{2,1,0:T(8,128)S(1)}, f32[2,256,256]{2,1,0:T(8,128)}, u32[]{:S(2)}, u32[]{:S(2)}) collective-permute-start(f32[2,256,256]{2,1,0:T(8,128)S(1)} %get-tuple-element.26), channel_id=1, source_target_pairs={{0,8},{4,12},{8,16},{12,20},{16,24},{20,28},{1,9},{5,13},{9,17},{1... | collective-permute-start | bytes 1572872 | tf_op jit(solution)/shard_map/ppermute | solution.py:19
  367.8 28.1 %collective-permute-start.11 = (f32[2,256,256]{2,1,0:T(8,128)}, f32[2,256,256]{2,1,0:T(8,128)}, u32[]{:S(2)}, u32[]{:S(2)}) collective-permute-start(f32[2,256,256]{2,1,0:T(8,128)} %get-tuple-element.25), channel_id=1, source_target_pairs={{0,12},{4,16},{8,20},{12,24},{16,28},{1,13},{5,17},{9,21},{13,25},... | collective-permute-start | bytes 1572872 | tf_op jit(solution)/shard_map/ppermute | solution.py:19
  372.1 23.9 %collective-permute-start.6 = (f32[2,256,256]{2,1,0:T(8,128)}, f32[2,256,256]{2,1,0:T(8,128)}, u32[]{:S(2)}, u32[]{:S(2)}) collective-permute-start(f32[2,256,256]{2,1,0:T(8,128)} %get-tuple-element.24), channel_id=1, source_target_pairs={{12,0},{16,4},{20,8},{24,12},{28,16},{13,1},{17,5},{21,9},{25,13},... | collective-permute-start | bytes 1572872 | tf_op jit(solution)/shard_map/ppermute | solution.py:19
  373.3 28.0 %collective-permute-start.7 = (f32[2,256,256]{2,1,0:T(8,128)}, f32[2,256,256]{2,1,0:T(8,128)}, u32[]{:S(2)}, u32[]{:S(2)}) collective-permute-start(f32[2,256,256]{2,1,0:T(8,128)} %get-tuple-element.29), channel_id=1, source_target_pairs={{8,0},{12,4},{16,8},{20,12},{24,16},{28,20},{9,1},{13,5},{17,9},{2... | collective-permute-start | bytes 1572872 | tf_op jit(solution)/shard_map/ppermute | solution.py:19
  374.6 26.7 %collective-permute-start.8 = (f32[2,256,256]{2,1,0:T(8,128)}, f32[2,256,256]{2,1,0:T(8,128)}, u32[]{:S(2)}, u32[]{:S(2)}) collective-permute-start(f32[2,256,256]{2,1,0:T(8,128)} %get-tuple-element.28), channel_id=1, source_target_pairs={{4,0},{8,4},{12,8},{16,12},{20,16},{24,20},{28,24},{5,1},{9,5},{13... | collective-permute-start | bytes 1572872 | tf_op jit(solution)/shard_map/ppermute | solution.py:19
  379.3 32.7 %collective-permute-start.9 = (f32[2,256,256]{2,1,0:T(8,128)}, f32[2,256,256]{2,1,0:T(8,128)}, u32[]{:S(2)}, u32[]{:S(2)}) collective-permute-start(f32[2,256,256]{2,1,0:T(8,128)} %get-tuple-element.27), channel_id=1, source_target_pairs={{0,4},{4,8},{8,12},{12,16},{16,20},{20,24},{24,28},{1,5},{5,9},{9,... | collective-permute-start | bytes 1572872 | tf_op jit(solution)/shard_map/ppermute | solution.py:19
  384.4 29.9 %copy-start.15 = (bf16[1024,3,256]{0,2,1:T(8,128)(2,1)S(1)}, bf16[1024,3,256]{0,2,1:T(8,128)(2,1)}, u32[]{:S(2)}) copy-start(bf16[1024,3,256]{0,2,1:T(8,128)(2,1)} %all-gather.4.cloned.1.call-done) | copy-start | bytes 4718596
  415.9 99.1 %reduce-scatter.10.cloned.1.call-start = ((), (), s32[]{:S(2)}) async-start(), calls=%async_computation.14 | async-start | bytes 36864 | tf_op jit(solution)/shard_map/reduce_scatter | solution.py:167
  460.0 122.2 %reduce-scatter.8.cloned.1.call-start = ((), (), s32[]{:S(2)}) async-start(), calls=%async_computation.13 | async-start | bytes 1179648 | tf_op jit(solution)/shard_map/reduce_scatter | solution.py:167
  461.4 199.0 %reduce-scatter.6.cloned.1.call-start = ((), (), s32[]{:S(2)}) async-start(), calls=%async_computation.12 | async-start | bytes 3538944 | tf_op jit(solution)/shard_map/reduce_scatter | solution.py:167
  464.0 287.9 %reduce-scatter.12.cloned.1.call-start = ((), (), s32[]{:S(2)}) async-start(), calls=%async_computation.15 | async-start | bytes 4718592 | tf_op jit(solution)/shard_map/reduce_scatter | solution.py:167
  467.8 376.8 %reduce-scatter.14.cloned.1.call-start = ((), (), s32[]{:S(2)}) async-start(), calls=%async_computation.16 | async-start | bytes 4718592 | tf_op jit(solution)/shard_map/reduce_scatter | solution.py:167
  472.1 22.1 %copy-start.9 = (f32[256,1024]{1,0:T(8,128)S(1)}, f32[256,1024]{1,0:T(8,128)}, u32[]{:S(2)}) copy-start(f32[256,1024]{1,0:T(8,128)} %all-reduce.11.cloned.1.call-done) | copy-start | bytes 3145732
  (13 other events, 24.0 us)
Sparse Core Ops, SparseCore 0:
  10.6 48.0 all-gather.3
  118.0 40.1 all-reduce.4
  160.5 51.4 all-gather.7
  214.1 47.4 all-gather.5
  267.8 34.5 all-reduce.8
  305.2 33.5 all-reduce.6
  416.0 41.5 all-reduce.10
  461.0 53.8 reduce-scatter.9
  519.3 62.8 reduce-scatter.7
  586.3 74.0 reduce-scatter.5
  664.6 87.1 reduce-scatter.11
  756.3 88.2 reduce-scatter.13
where the time goes:
time: 853 us; the launch traced here: 851 us
  waiting for transfers between devices  636 us (75%)
  blocking collectives  77.8 us (9%)
  matrix products  35.6 us (4%)
  starting transfers between devices  29.3 us (3%)
  local copies, waits for them, and re-layouts  29.2 us (3%)
  between operations  24.6 us (3%)
  other arithmetic  18.9 us (2%)
    reduce_scatter x5, waiting for transfers between devices, local_general(): lax.psum_scatter(v, 'seq', scatter_dimension=d, tiled=True)  348 us
    all_gather x2, blocking collectives, local_general(): cols = lambda v: lax.all_gather(v, 'seq', axis=1, tiled=True)  55.7 us
    all_gather x1, waiting for transfers between devices, local_general(): cols = lambda v: lax.all_gather(v, 'seq', axis=1, tiled=True)  52.1 us
    all_gather x2, waiting for transfers between devices, local_general(): rows = lambda v: lax.all_gather(v, 'seq', axis=0, tiled=True)  46.4 us
    ppermute x12, waiting for transfers between devices, shifted(): lax.ppermute(value, axis, [(i, i + steps) for i in range(first, last)])  42.2 us
    psum x1, waiting for transfers between devices, local_general(): lax.psum(jnp.einsum('tcf,dcf->td', grad_triple, qkv, preferred_element_ty...  41.7 us
    psum x1, waiting for transfers between devices, local_general(): middle = inputs + lax.psum(dot(attended, out_w, ((1,), (0,))), 'head')  38.9 us
    psum x1, waiting for transfers between devices, local_general(): lax.psum(dot(hidden, down_w, ((1,), (0,))).astype(BF16), 'head').astype(F32)  34.6 us
  transfers between devices with their start and end apart: 24, of which 17 were waited for; matrix products, arithmetic and copies ran while one was open for 4% of the time, Pallas kernels for 0%

commit v1 on v0

--- a/solution.py
+++ b/solution.py
@@ -11,6 +11,23 @@
 NEGATIVE = -1e30
 F32 = jnp.float32
 BF16 = jnp.bfloat16
+
+
+def settle_panel(vec):
+    y2 = lax.axis_size("seq")
+    x_next = lax.axis_index("seq")
+    m_next, z = (y2, x_next)
+    front, step_out = (vec, 1)
+    while step_out < m_next:
+        outcome_arr = range(m_next)
+        k_now = map(lambda it: (it, it ^ step_out), outcome_arr)
+        v1 = list(k_now)
+        local_now = lax.ppermute(front, axis_name="seq", perm=v1)
+        out_arr = jnp.concatenate([front, local_now], axis=1)
+        after = jnp.concatenate([local_now, front], axis=1)
+        front = jnp.where(z & step_out == 0, out_arr, after)
+        step_out = 2 * step_out
+    return front
 
 
 def shifted(value, axis, steps):
@@ -83,7 +100,7 @@
     tok, width = tokens.shape
     heads = w_qkv.shape[2] // HEAD_DIM
     rows = lambda v: lax.all_gather(v, "seq", axis=0, tiled=True)
-    cols = lambda v: lax.all_gather(v, "seq", axis=1, tiled=True)
+    cols = lambda v: settle_panel(v)
     vectors = jnp.stack([ln1_gain, ln1_bias, ln2_gain, ln2_bias, down_bias], axis=0)
     gain_one, shift_one, gain_two, shift_two, down_shift = [
         v[None].astype(F32) for v in cols(vectors)

time: 853 us -> 818 us (0.959)
  blocking collectives: 77.8 us -> 21.9 us
  starting transfers between devices: 29.3 us -> 50.3 us
  waiting for transfers between devices: 636 us -> 627 us
    all_gather x2 -> x0, blocking collectives: 55.7 us -> none  [local_general(): cols = lambda v: lax.all_gather(v, 'seq', axis=1, tiled=True)]
    all_gather x1 -> x0, waiting for transfers between devices: 52.1 us -> none  [local_general(): cols = lambda v: lax.all_gather(v, 'seq', axis=1, tiled=True)]
    all_gather x2, waiting for transfers between devices: 46.4 us -> 88.3 us  [local_general(): rows = lambda v: lax.all_gather(v, 'seq', axis=0, tiled=True)]
    psum x1, waiting for transfers between devices: 38.9 us -> 11.6 us  [local_general(): middle = inputs + lax.psum(dot(attended, out_w, ((1,), (0,))), 'head')]
    ppermute x0 -> x9, waiting for transfers between devices: none -> 20.6 us  [settle_panel(): local_now = lax.ppermute(front, axis_name='seq', perm=v1)]
    ppermute x0 -> x9, starting transfers between devices: none -> 16.6 us  [settle_panel(): local_now = lax.ppermute(front, axis_name='seq', perm=v1)]
    psum x1, waiting for transfers between devices: 41.7 us -> 56 us  [local_general(): lax.psum(jnp.einsum('tcf,dcf->td', grad_triple, qkv, preferred_element_ty...]
  transfers between devices with their start and end apart: 24 -> 32, of which waited for: 17 -> 22; matrix products, arithmetic and copies ran while one was open for 4% -> 6% of each run, Pallas kernels for 0% -> 0%
where the time goes in v1:
time: 818 us; the launch traced here: 817 us
  waiting for transfers between devices  627 us (77%)
  starting transfers between devices  50.3 us (6%)
  matrix products  40.5 us (5%)
  local copies, waits for them, and re-layouts  28.5 us (3%)
  between operations  24.4 us (3%)
  other arithmetic  23.6 us (3%)
  blocking collectives  21.9 us (3%)
    reduce_scatter x5, waiting for transfers between devices, local_general(): lax.psum_scatter(v, 'seq', scatter_dimension=d, tiled=True)  346 us
    all_gather x2, waiting for transfers between devices, local_general(): rows = lambda v: lax.all_gather(v, 'seq', axis=0, tiled=True)  88.3 us
    psum x1, waiting for transfers between devices, local_general(): lax.psum(jnp.einsum('tcf,dcf->td', grad_triple, qkv, preferred_element_ty...  56 us
    ppermute x12, waiting for transfers between devices, shifted(): lax.ppermute(value, axis, [(i, i + steps) for i in range(first, last)])  41 us
    ppermute x12, starting transfers between devices, shifted(): lax.ppermute(value, axis, [(i, i + steps) for i in range(first, last)])  33 us
    psum x1, waiting for transfers between devices, local_general(): lax.psum(dot(hidden, down_w, ((1,), (0,))).astype(BF16), 'head').astype(F32)  32.9 us
    psum x1, waiting for transfers between devices, local_general(): grad_two = lax.psum(dot(grad_pre, up_w, ((1,), (1,))), 'head')  30 us
    dot_general x9, matrix products, dot(): return lax.dot_general(a, b, (dims, ((), ())), preferred_element_type=F32)  25.3 us
  transfers between devices with their start and end apart: 32, of which 22 were waited for; matrix products, arithmetic and copies ran while one was open for 6% of the time, Pallas kernels for 0%

profile of v1, /device:TPU:0, one launch (start us, length us, event | category | flops | bytes accessed | tf_op | source)
XLA Modules:
  0.0 816.7 jit_solution(5098405033179958429)
XLA Ops:
  8.0 3.0 collective-permute-start
  37.2 21.7 %all-gather.3.cloned.1.call-done = bf16[1024,3,256]{0,2,1:T(8,128)(2,1)} async-done(((bf16[128,3,256]{0,2,1:T(8,128)(2,1)}), bf16[1024,3,256]{0,2,1:T(8,128)(2,1)}) %all-gather.3.cloned.1.call-update) | async-done | bytes 1572880 | tf_op jit(solution)/shard_map/all_gather | solution.py:102
  63.2 3.9 collective-permute-start.4
  67.3 3.3 collective-permute-start.5
  79.9 10.6 %collective-permute-done.7 = bf16[2,256,256]{1,2,0:T(8,128)(2,1)S(1)} collective-permute-done((bf16[2,256,256]{1,2,0:T(8,128)(2,1)S(1)}, bf16[2,256,256]{1,2,0:T(8,128)(2,1)S(1)}, u32[]{:S(2)}, u32[]{:S(2)}) %collective-permute-start.7) | collective-permute-done | bytes 262176 | tf_op jit(solution)/shard_map/ppermute | solution.py:36
  90.5 6.0 collective-permute-done.8
  98.2 2.9 fusion.53
  101.9 3.2 convolution_convert_fusion.3
  108.4 8.3 %collective-permute-start.12 = (bf16[1024,128]{1,0:T(8,128)(2,1)S(1)}, bf16[1024,128]{1,0:T(8,128)(2,1)S(1)}, u32[]{:S(2)}, u32[]{:S(2)}) collective-permute-start(bf16[1024,128]{1,0:T(8,128)(2,1)S(1)} %copy-done.17), channel_id=1, source_target_pairs={{0,4},{4,0},{8,12},{12,8},{16,20},{20,16},{24,28},{28,24},{1,5},{5... | collective-permute-start | bytes 786440 | tf_op jit(solution)/shard_map/ppermute | solution.py:25
  116.7 6.0 collective-permute-done.12
  123.0 12.8 %collective-permute-done.13 = bf16[1024,256]{1,0:T(8,128)(2,1)S(1)} collective-permute-done((bf16[1024,256]{1,0:T(8,128)(2,1)S(1)}, bf16[1024,256]{1,0:T(8,128)(2,1)S(1)}, u32[]{:S(2)}, u32[]{:S(2)}) %collective-permute-start.13) | collective-permute-done | bytes 524320 | tf_op jit(solution)/shard_map/ppermute | solution.py:25
  137.2 11.6 %all-reduce.5.cloned.1.call-done = f32[256,1024]{1,0:T(8,128)} async-done(((f32[256,1024]{1,0:T(8,128)}), f32[256,1024]{1,0:T(8,128)}) %all-reduce.5.cloned.1.call-update) | async-done | bytes 1048592 | tf_op jit(solution)/shard_map/psum | solution.py:136
  150.5 66.6 %all-gather.5.cloned.1.call-done = bf16[1024,1024]{1,0:T(8,128)(2,1)} async-done(((bf16[128,1024]{1,0:T(8,128)(2,1)}), bf16[1024,1024]{1,0:T(8,128)(2,1)}) %all-gather.5.cloned.1.call-update) | async-done | bytes 2097168 | tf_op jit(solution)/shard_map/all_gather | solution.py:102
  219.5 4.6 convert_reduce_fusion.2
  226.1 4.5 convolution_convert_fusion
  230.7 30.0 %all-reduce.9.cloned.1.call-done = f32[256,1024]{1,0:T(8,128)} async-done(((f32[256,1024]{1,0:T(8,128)}), f32[256,1024]{1,0:T(8,128)}) %all-reduce.9.cloned.1.call-update) | async-done | bytes 1048592 | tf_op jit(solution)/shard_map/psum | solution.py:149
  264.1 32.9 %all-reduce.7.cloned.1.call-done = bf16[256,1024]{1,0:T(8,128)(2,1)} async-done(((bf16[256,1024]{1,0:T(8,128)(2,1)}), bf16[256,1024]{1,0:T(8,128)(2,1)}) %all-reduce.7.cloned.1.call-update) | async-done | bytes 524304 | tf_op jit(solution)/shard_map/psum | solution.py:142
  297.0 3.5 convert_add_fusion.1
  327.2 5.4 collective-permute-start.18
  332.5 4.7 collective-permute-start.19
  337.2 3.9 collective-permute-done.15
  341.1 6.0 collective-permute-start.20
  348.0 3.5 collective-permute-done.16
  351.5 11.7 %collective-permute-done.18 = f32[2,256,256]{2,1,0:T(8,128)} collective-permute-done((f32[2,256,256]{2,1,0:T(8,128)}, f32[2,256,256]{2,1,0:T(8,128)}, u32[]{:S(2)}, u32[]{:S(2)}) %collective-permute-start.18) | collective-permute-done | bytes 524320 | tf_op jit(solution)/shard_map/ppermute | solution.py:36
  367.1 56.0 %all-reduce.11.cloned.1.call-done = f32[256,1024]{1,0:T(8,128)} async-done(((f32[256,1024]{1,0:T(8,128)}), f32[256,1024]{1,0:T(8,128)}) %all-reduce.11.cloned.1.call-update) | async-done | bytes 1048592 | tf_op jit(solution)/shard_map/psum | solution.py:170
  434.3 4.1 fusion.47
  439.2 21.9 %psum.39 = f32[1024]{0:T(1024)} all-reduce(f32[1024]{0:T(1024)S(1)} %copy-done.35), channel_id=1, replica_groups=mesh['seq'=8,'head'=4] {'seq'}, use_global_device_ids=true, to_apply=%region_25.26 | all-reduce | flops 1024 | bytes 8192 | tf_op jit(solution)/shard_map/psum | solution.py:148
  462.5 18.0 %reduce-scatter.10.cloned.1.call-done = f32[5,128]{1,0:T(8,128)} async-done(((f32[5,1024]{1,0:T(8,128)}), f32[5,128]{1,0:T(8,128)}) %reduce-scatter.10.cloned.1.call-update) | async-done | bytes 2576 | tf_op jit(solution)/shard_map/reduce_scatter | solution.py:184
  481.8 65.9 %reduce-scatter.8.cloned.1.call-done = f32[256,128]{1,0:T(8,128)} async-done(((f32[256,1024]{1,0:T(8,128)}), f32[256,128]{1,0:T(8,128)}) %reduce-scatter.8.cloned.1.call-update) | async-done | bytes 131088 | tf_op jit(solution)/shard_map/reduce_scatter | solution.py:184
  547.8 78.3 %reduce-scatter.6.cloned.1.call-done = f32[128,3,256]{2,0,1:T(8,128)} async-done(((f32[1024,3,256]{2,0,1:T(8,128)}), f32[128,3,256]{2,0,1:T(8,128)}) %reduce-scatter.6.cloned.1.call-update) | async-done | bytes 393232 | tf_op jit(solution)/shard_map/reduce_scatter | solution.py:184
  626.1 91.1 %reduce-scatter.12.cloned.1.call-done = f32[128,1024]{1,0:T(8,128)} async-done(((f32[1024,1024]{1,0:T(8,128)}), f32[128,1024]{1,0:T(8,128)}) %reduce-scatter.12.cloned.1.call-update) | async-done | bytes 524304 | tf_op jit(solution)/shard_map/reduce_scatter | solution.py:184
  717.2 92.9 %reduce-scatter.14.cloned.1.call-done = f32[1024,128]{1,0:T(8,128)} async-done(((f32[1024,1024]{1,0:T(8,128)}), f32[1024,128]{1,0:T(8,128)}) %reduce-scatter.14.cloned.1.call-update) | async-done | bytes 524304 | tf_op jit(solution)/shard_map/reduce_scatter | solution.py:184
  (208 shorter events, 93.3 us)
Async XLA Ops:
  7.2 51.7 %all-gather.3.cloned.1.call-start = ((), (), s32[]{:S(2)}) async-start(), calls=%async_computation.5 | async-start | bytes 1769472 | tf_op jit(solution)/shard_map/all_gather | solution.py:102
  8.0 17.4 %collective-permute-start = (bf16[5,128]{1,0:T(8,128)(2,1)S(1)}, bf16[5,128]{1,0:T(8,128)(2,1)S(1)}, u32[]{:S(2)}, u32[]{:S(2)}) collective-permute-start(bf16[5,128]{1,0:T(8,128)(2,1)S(1)} %stack.75), channel_id=1, source_target_pairs={{0,4},{4,0},{8,12},{12,8},{16,20},{20,16},{24,28},{28,24},{1,5},{5... | collective-permute-start | bytes 3848 | tf_op jit(solution)/shard_map/ppermute | solution.py:25
  12.8 136.0 %all-reduce.5.cloned.1.call-start = ((), (), s32[]{:S(2)}) async-start(), calls=%async_computation.6 | async-start | bytes 2097152 | tf_op jit(solution)/shard_map/psum | solution.py:136
  12.9 23.9 %collective-permute-start.9 = (bf16[256,128]{1,0:T(8,128)(2,1)}, bf16[256,128]{1,0:T(8,128)(2,1)S(1)}, u32[]{:S(2)}, u32[]{:S(2)}) collective-permute-start(bf16[256,128]{1,0:T(8,128)(2,1)} %param.17), channel_id=1, source_target_pairs={{0,4},{4,0},{8,12},{12,8},{16,20},{20,16},{24,28},{28,24},{1,5},{5... | collective-permute-start | bytes 196616 | tf_op jit(solution)/shard_map/ppermute | solution.py:25
  25.4 6.1 collective-permute-start.1
  31.6 4.6 collective-permute-start.2
  36.9 30.2 %collective-permute-start.10 = (bf16[256,256]{1,0:T(8,128)(2,1)S(1)}, bf16[256,256]{1,0:T(8,128)(2,1)S(1)}, u32[]{:S(2)}, u32[]{:S(2)}) collective-permute-start(bf16[256,256]{1,0:T(8,128)(2,1)S(1)} %maximum_select_fusion.7), channel_id=1, source_target_pairs={{0,8},{4,12},{8,0},{12,4},{16,24},{20,28},{24,16},{28,20},{1,9},{5... | collective-permute-start | bytes 393224 | tf_op jit(solution)/shard_map/ppermute | solution.py:25
  61.2 10.8 %collective-permute-start.3 = (bf16[2,256,256]{1,2,0:T(8,128)(2,1)S(1)}, bf16[2,256,256]{1,2,0:T(8,128)(2,1)S(1)}, u32[]{:S(2)}, u32[]{:S(2)}) collective-permute-start(bf16[2,256,256]{1,2,0:T(8,128)(2,1)S(1)} %pad_maximum_fusion.1), channel_id=1, source_target_pairs={{0,12},{4,16},{8,20},{12,24},{16,28},{1,13},{5,17},{9,21},{13,25},... | collective-permute-start | bytes 786440 | tf_op jit(solution)/shard_map/ppermute | solution.py:36
  63.2 11.9 %collective-permute-start.4 = (bf16[2,256,256]{1,2,0:T(8,128)(2,1)S(1)}, bf16[2,256,256]{1,2,0:T(8,128)(2,1)S(1)}, u32[]{:S(2)}, u32[]{:S(2)}) collective-permute-start(bf16[2,256,256]{1,2,0:T(8,128)(2,1)S(1)} %pad_maximum_fusion.1), channel_id=1, source_target_pairs={{0,8},{4,12},{8,16},{12,20},{16,24},{20,28},{1,9},{5,13},{9,17},{1... | collective-permute-start | bytes 786440 | tf_op jit(solution)/shard_map/ppermute | solution.py:36
  67.2 37.9 %collective-permute-start.11 = (bf16[256,512]{1,0:T(8,128)(2,1)S(1)}, bf16[256,512]{1,0:T(8,128)(2,1)}, u32[]{:S(2)}, u32[]{:S(2)}) collective-permute-start(bf16[256,512]{1,0:T(8,128)(2,1)S(1)} %maximum_select_fusion.6), channel_id=1, source_target_pairs={{0,16},{4,20},{8,24},{12,28},{16,0},{20,4},{24,8},{28,12},{1,17},{... | collective-permute-start | bytes 786440 | tf_op jit(solution)/shard_map/ppermute | solution.py:25
  67.3 10.1 %collective-permute-start.5 = (bf16[2,256,256]{1,2,0:T(8,128)(2,1)S(1)}, bf16[2,256,256]{1,2,0:T(8,128)(2,1)S(1)}, u32[]{:S(2)}, u32[]{:S(2)}) collective-permute-start(bf16[2,256,256]{1,2,0:T(8,128)(2,1)S(1)} %pad_maximum_fusion.1), channel_id=1, source_target_pairs={{0,4},{4,8},{8,12},{12,16},{16,20},{20,24},{24,28},{1,5},{5,9},{9,... | collective-permute-start | bytes 786440 | tf_op jit(solution)/shard_map/ppermute | solution.py:36
  70.6 9.3 %collective-permute-start.6 = (bf16[2,256,256]{1,2,0:T(8,128)(2,1)S(1)}, bf16[2,256,256]{1,2,0:T(8,128)(2,1)S(1)}, u32[]{:S(2)}, u32[]{:S(2)}) collective-permute-start(bf16[2,256,256]{1,2,0:T(8,128)(2,1)S(1)} %pad_maximum_fusion.1), channel_id=1, source_target_pairs={{4,0},{8,4},{12,8},{16,12},{20,16},{24,20},{28,24},{5,1},{9,5},{13... | collective-permute-start | bytes 786440 | tf_op jit(solution)/shard_map/ppermute | solution.py:36
  72.0 18.6 %collective-permute-start.7 = (bf16[2,256,256]{1,2,0:T(8,128)(2,1)S(1)}, bf16[2,256,256]{1,2,0:T(8,128)(2,1)S(1)}, u32[]{:S(2)}, u32[]{:S(2)}) collective-permute-start(bf16[2,256,256]{1,2,0:T(8,128)(2,1)S(1)} %pad_maximum_fusion.1), channel_id=1, source_target_pairs={{8,0},{12,4},{16,8},{20,12},{24,16},{28,20},{9,1},{13,5},{17,9},{2... | collective-permute-start | bytes 786440 | tf_op jit(solution)/shard_map/ppermute | solution.py:36
  75.1 21.5 %collective-permute-start.8 = (bf16[2,256,256]{1,2,0:T(8,128)(2,1)S(1)}, bf16[2,256,256]{1,2,0:T(8,128)(2,1)S(1)}, u32[]{:S(2)}, u32[]{:S(2)}) collective-permute-start(bf16[2,256,256]{1,2,0:T(8,128)(2,1)S(1)} %pad_maximum_fusion.1), channel_id=1, source_target_pairs={{12,0},{16,4},{20,8},{24,12},{28,16},{13,1},{17,5},{21,9},{25,13},... | collective-permute-start | bytes 786440 | tf_op jit(solution)/shard_map/ppermute | solution.py:36
  107.6 109.4 %all-gather.5.cloned.1.call-start = ((), (), s32[]{:S(2)}) async-start(), calls=%async_computation.7 | async-start | bytes 2359296 | tf_op jit(solution)/shard_map/all_gather | solution.py:102
  108.3 152.3 %all-reduce.9.cloned.1.call-start = ((), (), s32[]{:S(2)}) async-start(), calls=%async_computation.9 | async-start | bytes 2097152 | tf_op jit(solution)/shard_map/psum | solution.py:149
  108.4 14.3 %collective-permute-start.12 = (bf16[1024,128]{1,0:T(8,128)(2,1)S(1)}, bf16[1024,128]{1,0:T(8,128)(2,1)S(1)}, u32[]{:S(2)}, u32[]{:S(2)}) collective-permute-start(bf16[1024,128]{1,0:T(8,128)(2,1)S(1)} %copy-done.17), channel_id=1, source_target_pairs={{0,4},{4,0},{8,12},{12,8},{16,20},{20,16},{24,28},{28,24},{1,5},{5... | collective-permute-start | bytes 786440 | tf_op jit(solution)/shard_map/ppermute | solution.py:25
  122.9 12.9 %collective-permute-start.13 = (bf16[1024,256]{1,0:T(8,128)(2,1)S(1)}, bf16[1024,256]{1,0:T(8,128)(2,1)S(1)}, u32[]{:S(2)}, u32[]{:S(2)}) collective-permute-start(bf16[1024,256]{1,0:T(8,128)(2,1)S(1)} %maximum_select_fusion.3), channel_id=1, source_target_pairs={{0,8},{4,12},{8,0},{12,4},{16,24},{20,28},{24,16},{28,20},{1,9},{5... | collective-permute-start | bytes 1572872 | tf_op jit(solution)/shard_map/ppermute | solution.py:25
  137.2 82.3 %collective-permute-start.14 = (bf16[1024,512]{1,0:T(8,128)(2,1)}, bf16[1024,512]{1,0:T(8,128)(2,1)}, u32[]{:S(2)}, u32[]{:S(2)}) collective-permute-start(bf16[1024,512]{1,0:T(8,128)(2,1)} %maximum_select_fusion.1), channel_id=1, source_target_pairs={{0,16},{4,20},{8,24},{12,28},{16,0},{20,4},{24,8},{28,12},{1,17},{... | collective-permute-start | bytes 3145736 | tf_op jit(solution)/shard_map/ppermute | solution.py:25
  225.9 71.1 %all-reduce.7.cloned.1.call-start = ((), (), s32[]{:S(2)}) async-start(), calls=%async_computation.8 | async-start | bytes 1048576 | tf_op jit(solution)/shard_map/psum | solution.py:142
  230.6 192.5 %all-reduce.11.cloned.1.call-start = ((), (), s32[]{:S(2)}) async-start(), calls=%async_computation.10 | async-start | bytes 2097152 | tf_op jit(solution)/shard_map/psum | solution.py:170
  323.3 17.8 %collective-permute-start.15 = (f32[2,256,256]{2,1,0:T(8,128)S(1)}, f32[2,256,256]{2,1,0:T(8,128)}, u32[]{:S(2)}, u32[]{:S(2)}) collective-permute-start(f32[2,256,256]{2,1,0:T(8,128)S(1)} %get-tuple-element.22), channel_id=1, source_target_pairs={{12,0},{16,4},{20,8},{24,12},{28,16},{13,1},{17,5},{21,9},{25,13},... | collective-permute-start | bytes 1572872 | tf_op jit(solution)/shard_map/ppermute | solution.py:36
  324.6 26.9 %collective-permute-start.16 = (f32[2,256,256]{2,1,0:T(8,128)}, f32[2,256,256]{2,1,0:T(8,128)}, u32[]{:S(2)}, u32[]{:S(2)}) collective-permute-start(f32[2,256,256]{2,1,0:T(8,128)} %get-tuple-element.27), channel_id=1, source_target_pairs={{8,0},{12,4},{16,8},{20,12},{24,16},{28,20},{9,1},{13,5},{17,9},{2... | collective-permute-start | bytes 1572872 | tf_op jit(solution)/shard_map/ppermute | solution.py:36
  325.9 25.6 %collective-permute-start.17 = (f32[2,256,256]{2,1,0:T(8,128)}, f32[2,256,256]{2,1,0:T(8,128)}, u32[]{:S(2)}, u32[]{:S(2)}) collective-permute-start(f32[2,256,256]{2,1,0:T(8,128)} %get-tuple-element.26), channel_id=1, source_target_pairs={{4,0},{8,4},{12,8},{16,12},{20,16},{24,20},{28,24},{5,1},{9,5},{13... | collective-permute-start | bytes 1572872 | tf_op jit(solution)/shard_map/ppermute | solution.py:36
  327.2 36.0 %collective-permute-start.18 = (f32[2,256,256]{2,1,0:T(8,128)}, f32[2,256,256]{2,1,0:T(8,128)}, u32[]{:S(2)}, u32[]{:S(2)}) collective-permute-start(f32[2,256,256]{2,1,0:T(8,128)} %get-tuple-element.25), channel_id=1, source_target_pairs={{0,4},{4,8},{8,12},{12,16},{16,20},{20,24},{24,28},{1,5},{5,9},{9,... | collective-permute-start | bytes 1572872 | tf_op jit(solution)/shard_map/ppermute | solution.py:36
  332.5 30.7 %collective-permute-start.19 = (f32[2,256,256]{2,1,0:T(8,128)}, f32[2,256,256]{2,1,0:T(8,128)}, u32[]{:S(2)}, u32[]{:S(2)}) collective-permute-start(f32[2,256,256]{2,1,0:T(8,128)} %get-tuple-element.24), channel_id=1, source_target_pairs={{0,8},{4,12},{8,16},{12,20},{16,24},{20,28},{1,9},{5,13},{9,17},{1... | collective-permute-start | bytes 1572872 | tf_op jit(solution)/shard_map/ppermute | solution.py:36
  341.1 22.1 %collective-permute-start.20 = (f32[2,256,256]{2,1,0:T(8,128)}, f32[2,256,256]{2,1,0:T(8,128)}, u32[]{:S(2)}, u32[]{:S(2)}) collective-permute-start(f32[2,256,256]{2,1,0:T(8,128)} %get-tuple-element.23), channel_id=1, source_target_pairs={{0,12},{4,16},{8,20},{12,24},{16,28},{1,13},{5,17},{9,21},{13,25},... | collective-permute-start | bytes 1572872 | tf_op jit(solution)/shard_map/ppermute | solution.py:36
  367.1 113.3 %reduce-scatter.10.cloned.1.call-start = ((), (), s32[]{:S(2)}) async-start(), calls=%async_computation.13 | async-start | bytes 36864 | tf_op jit(solution)/shard_map/reduce_scatter | solution.py:184
  425.6 122.2 %reduce-scatter.8.cloned.1.call-start = ((), (), s32[]{:S(2)}) async-start(), calls=%async_computation.12 | async-start | bytes 1179648 | tf_op jit(solution)/shard_map/reduce_scatter | solution.py:184
  426.9 199.2 %reduce-scatter.6.cloned.1.call-start = ((), (), s32[]{:S(2)}) async-start(), calls=%async_computation.11 | async-start | bytes 3538944 | tf_op jit(solution)/shard_map/reduce_scatter | solution.py:184
  429.5 287.8 %reduce-scatter.12.cloned.1.call-start = ((), (), s32[]{:S(2)}) async-start(), calls=%async_computation.14 | async-start | bytes 4718592 | tf_op jit(solution)/shard_map/reduce_scatter | solution.py:184
  433.3 376.8 %reduce-scatter.14.cloned.1.call-start = ((), (), s32[]{:S(2)}) async-start(), calls=%async_computation.15 | async-start | bytes 4718592 | tf_op jit(solution)/shard_map/reduce_scatter | solution.py:184
  (37 other events, 911.1 us)
Sparse Core Ops, SparseCore 0:
  13.0 45.9 all-gather.2
  107.7 41.0 all-reduce.4
  151.1 65.8 all-gather.4
  226.0 34.5 all-reduce.8
  263.4 33.5 all-reduce.6
  367.2 55.8 all-reduce.10
  426.5 53.8 reduce-scatter.9
  484.8 62.9 reduce-scatter.7
  551.9 74.0 reduce-scatter.5
  630.1 87.0 reduce-scatter.11
  721.9 88.2 reduce-scatter.13
